TPU v7x, 256 devices: a whole 4x4x8 slice. The times are simulated.
256 devices in a mesh: dp: 4 (over y), mp: 64 (over x, z, core).
Axes of the slice: x: 4, y: 4, z: 8, core: 2. Of those that a mesh axis runs over, the one named last changes fastest.
Arguments:
- inputs: bfloat16 [8, 256, 6144], P('dp', None, 'mp'), may hold values from -6 to 6
- cotangent: bfloat16 [8, 256, 6144], P('dp', None, 'mp'), may hold values from -6 to 6
- w_up: bfloat16 [6144, 24576], P('dp', 'mp'), may hold values from -0.078125 to 0.078125
- w_down: bfloat16 [24576, 6144], P('mp', 'dp'), may hold values from -0.0390625 to 0.0390625
- thresholds: float32 [2], replicated, may hold values from 23592.96 to 58982.4
Outputs:
- grad_up: float32 [6144, 24576], P('dp', 'mp')
- grad_down: float32 [24576, 6144], P('mp', 'dp')
- norms: float32 [8, 2], P('dp')
All inputs are finite; a program needn't handle non-finite values.
Results may differ from a plain program's by a relative error of at most 0.0085.
Values may be sent and summed in bfloat16 or wider, within the bound.
A program may use at most 128 MiB of HBM per device.

v0:
```python
import jax
import jax.numpy as jnp
from jax import lax
from jax.sharding import PartitionSpec as P

inv_root_two = 0.7071067811865476
inv_root_two_pi = 0.3989422804014327


def sent_to_all(shard, axis):
    copies = jnp.broadcast_to(shard, (lax.axis_size(axis), *shard.shape))
    return lax.all_to_all(copies, axis, split_axis=0, concat_axis=0, tiled=True)


def taken_together(shard, axis):
    return sent_to_all(shard, axis).sum(axis=0)


def packed_total(arrays, axis):
    line, at, outs = (jnp.concatenate([a.reshape(-1) for a in arrays]), 0, [])
    running = taken_together(line, axis)
    for a in arrays:
        outs.append(running[at : at + a.size].reshape(a.shape))
        at += a.size
    return tuple(outs)


def split_up(shard, dim, count):
    shape = shard.shape
    pieces = shard.reshape(*shape[:dim], count, shape[dim] // count, *shape[dim + 1 :])
    return jnp.moveaxis(pieces, dim, 0)


def sum_at_owner(shard, axis, dim):
    pieces = split_up(shard, dim, lax.axis_size(axis))
    arrived = lax.all_to_all(pieces, axis, split_axis=0, concat_axis=0, tiled=True)
    return arrived.astype(jnp.float32).sum(axis=0)


def normal_cdf(value):
    return 0.5 * (1.0 + lax.erf(value * inv_root_two))


def gram_of(array, images, patches):
    cube = array.reshape(images, patches, -1)
    return jnp.einsum("btd,bsd->bts", cube, cube, preferred_element_type=jnp.float32)


def on_device(inputs, cotangent, w_up, w_down, thresholds):
    images, patches, local_feats = inputs.shape
    count_rows = images * patches
    x_whole = lax.all_gather(inputs, "mp", axis=2, tiled=True).reshape(count_rows, -1)
    hidden_local = w_up.shape[1]
    columns = x_whole
    pre = jnp.dot(
        columns, lax.all_gather(w_up, "dp", axis=0, tiled=True), preferred_element_type=jnp.float32
    )
    act = (pre * normal_cdf(pre)).astype(jnp.bfloat16)
    dy_whole = lax.all_gather(cotangent, "mp", axis=2, tiled=True).reshape(count_rows, -1)
    columns = dy_whole
    dact = lax.dot_general(
        columns,
        lax.all_gather(w_down, "dp", axis=1, tiled=True),
        (((1,), (1,)), ((), ())),
        preferred_element_type=jnp.float32,
    )
    slope = normal_cdf(pre) + pre * jnp.exp(-0.5 * pre * pre) * inv_root_two_pi
    dpre = (dact * slope).astype(jnp.bfloat16)
    gram_dpre = gram_of(dpre, images, patches)
    gram_act = gram_of(act, images, patches)
    part_up = jnp.sum(gram_of(x_whole, images, patches) * gram_dpre, axis=(1, 2))
    part_down = jnp.sum(gram_act * gram_of(dy_whole, images, patches), axis=(1, 2))
    sq_up, sq_down = packed_total((part_up, part_down), "mp")
    norms = jnp.stack([jnp.sqrt(sq_up), jnp.sqrt(sq_down)], axis=1)
    factor = jnp.minimum(1.0, thresholds[None, :] / (norms + 1e-06))
    dpre_clip = (
        (
            factor[:, 0][:, None, None]
            * dpre.reshape(images, patches, hidden_local).astype(jnp.float32)
        )
        .astype(jnp.bfloat16)
        .reshape(count_rows, hidden_local)
    )
    cot_clip = (
        (factor[:, 1][:, None, None] * dy_whole.reshape(images, patches, -1).astype(jnp.float32))
        .astype(jnp.bfloat16)
        .reshape(count_rows, -1)
    )
    columns = x_whole
    grad_up = lax.psum_scatter(
        lax.dot_general(
            columns, dpre_clip, (((0,), (0,)), ((), ())), preferred_element_type=jnp.float32
        ).astype(jnp.bfloat16),
        "dp",
        scatter_dimension=0,
        tiled=True,
    ).astype(jnp.float32)
    down_full = lax.dot_general(
        act, cot_clip, (((0,), (0,)), ((), ())), preferred_element_type=jnp.float32
    )
    grad_down = sum_at_owner(down_full.astype(jnp.bfloat16), "dp", 1)
    return (grad_up, grad_down, norms)


def solution(mesh):
    in_specs = (P("dp", None, "mp"), P("dp", None, "mp"), P("dp", "mp"), P("mp", "dp"), P())
    out_specs = (P("dp", "mp"), P("mp", "dp"), P("dp", None))
    return jax.shard_map(
        on_device, mesh=mesh, in_specs=in_specs, out_specs=out_specs, check_vma=False
    )
```

profile of v0, /device:TPU:1, one launch (start us, length us, event | category | flops | bytes accessed | tf_op | source)
XLA Modules:
  0.0 445.1 jit_solution(11769768210793305239)
XLA Ops:
  7.2 0.0 all-gather.5.cloned.1.call-start
  7.2 0.7 all-gather.5.cloned.1.call-update
  7.9 0.0 all-gather.7.cloned.1.call-start
  7.9 0.7 all-gather.7.cloned.1.call-update
  8.6 0.0 all-gather.11.cloned.1.call-start
  8.7 0.7 all-gather.11.cloned.1.call-update
  9.4 0.0 all-gather.9.cloned.1.call-start
  9.4 0.5 all-gather.9.cloned.1.call-update
  10.0 85.6 %all-gather.5.cloned.1.call-done = bf16[2,256,6144]{1,2,0:T(8,128)(2,1)} async-done(((bf16[2,256,96]{1,2,0:T(8,128)(2,1)}), bf16[2,256,6144]{1,2,0:T(8,128)(2,1)}) %all-gather.5.cloned.1.call-update) | async-done | bytes 6291472 | tf_op jit(solution)/shard_map/all_gather | solution.py:52
  95.5 8.7 %copy.32 = bf16[2,256,6144]{2,1,0:T(8,128)(2,1)} copy(bf16[2,256,6144]{1,2,0:T(8,128)(2,1)} %all-gather.5.cloned.1.call-done) | data formatting | bytes 12582912 | tf_op jit(solution)/shard_map/all_gather | solution.py:52
  104.2 71.4 %all-gather.7.cloned.1.call-done = bf16[2,256,6144]{1,2,0:T(8,128)(2,1)} async-done(((bf16[2,256,96]{1,2,0:T(8,128)(2,1)}), bf16[2,256,6144]{1,2,0:T(8,128)(2,1)}) %all-gather.7.cloned.1.call-update) | async-done | bytes 6291472 | tf_op jit(solution)/shard_map/all_gather | solution.py:59
  175.6 8.7 %copy.31 = bf16[2,256,6144]{2,1,0:T(8,128)(2,1)} copy(bf16[2,256,6144]{1,2,0:T(8,128)(2,1)} %all-gather.7.cloned.1.call-done) | data formatting | bytes 12582912 | tf_op jit(solution)/shard_map/all_gather | solution.py:59
  184.3 44.5 %all-gather.11.cloned.1.call-done = bf16[6144,384]{1,0:T(8,128)(2,1)} async-done(((bf16[1536,384]{1,0:T(8,128)(2,1)}), bf16[6144,384]{1,0:T(8,128)(2,1)}) %all-gather.11.cloned.1.call-update) | async-done | bytes 4718608 | tf_op jit(solution)/shard_map/all_gather | solution.py:56
  228.8 7.0 %multiply_convert_fusion.2 = (bf16[512,384]{1,0:T(8,128)(2,1)S(1)}, f32[512,384]{1,0:T(8,128)S(1)}) fusion(bf16[512,6144]{1,0:T(8,128)(2,1)} %bitcast.47, bf16[6144,384]{1,0:T(8,128)(2,1)} %all-gather.11.cloned.1.call-done), kind=kOutput, calls=%fused_computation.18 | convolution fusion | flops 2416902144 | bytes 12189696 | tf_op jit(solution)/shard_map/dot_general | solution.py:55
  235.7 50.3 %all-gather.9.cloned.1.call-done = bf16[384,6144]{1,0:T(8,128)(2,1)} async-done(((bf16[384,1536]{1,0:T(8,128)(2,1)}), bf16[384,6144]{1,0:T(8,128)(2,1)}) %all-gather.9.cloned.1.call-update) | async-done | bytes 4718608 | tf_op jit(solution)/shard_map/all_gather | solution.py:63
  286.0 7.7 %fusion.1 = bf16[512,384]{1,0:T(8,128)(2,1)S(1)} fusion(bf16[512,6144]{1,0:T(8,128)(2,1)} %bitcast.46, bf16[384,6144]{1,0:T(8,128)(2,1)} %all-gather.9.cloned.1.call-done, f32[512,384]{1,0:T(8,128)S(1)} %get-tuple-element.25), kind=kOutput, calls=%fused_computation.7 | convolution fusion | flops 2417885184 | bytes 12189696 | tf_op jit(solution)/shard_map/dot_general | solution.py:61
  293.7 0.3 fusion.9
  294.0 0.0 slice-start
  294.0 0.3 fusion.10
  294.4 0.0 slice-start.1
  294.4 7.4 %fusion.2 = f32[2]{0:T(128)S(1)} fusion(f32[2,256,256]{2,1,0:T(8,128)S(1)} %fusion.9, bf16[2,256,6144]{1,2,0:T(8,128)(2,1)} %all-gather.5.cloned.1.call-done), kind=kOutput, calls=%fused_computation.11 | convolution fusion | flops 1610874880 | bytes 6815752 | tf_op jit(solution)/shard_map/btd,bsd->bts/dot_general | solution.py:46
  301.8 0.0 slice-done
  301.8 0.0 slice-done.1
  301.8 0.0 copy-start
  301.8 2.7 fusion.3
  304.5 0.1 pad_maximum_fusion.1
  304.6 0.6 broadcast_in_dim.4
  305.2 10.8 %all-to-all-start = ((f32[64,1,4]{2,1,0:T(1,128)}), f32[64,1,4]{2,1,0:T(1,128)S(1)}, u32[]{:S(2)}, u32[]{:S(2)}) async-start(f32[64,1,4]{2,1,0:T(1,128)} %broadcast_in_dim.4), calls=%async_computation | async-start | bytes 65536 | tf_op jit(solution)/shard_map/all_to_all | solution.py:12
  316.1 0.2 reduce-scatter.2.cloned.1.call-start
  316.3 0.2 copy.34
  316.5 8.8 %all-to-all-done = f32[64,1,4]{2,1,0:T(1,128)S(1)} async-done(((f32[64,1,4]{2,1,0:T(1,128)}), f32[64,1,4]{2,1,0:T(1,128)S(1)}, u32[]{:S(2)}, u32[]{:S(2)}) %all-to-all-start) | async-done | bytes 1056 | tf_op jit(solution)/shard_map/all_to_all | solution.py:12
  325.3 0.1 reduce_sum.38
  325.4 0.1 sqrt_bitcast_fusion.1
  325.5 0.0 copy-done
  325.5 0.1 pad_maximum_fusion
  325.5 8.6 %fusion = bf16[6144,384]{0,1:T(8,128)(2,1)} fusion(bf16[2,256,6144]{1,2,0:T(8,128)(2,1)} %all-gather.5.cloned.1.call-done, bf16[2,256,384]{1,2,0:T(8,128)(2,1)S(1)} %copy.34, f32[2]{0:T(128)S(1)} %get-tuple-element.21), kind=kOutput, calls=%fused_computation.4 | convolution fusion | flops 2418868224 | bytes 11403272 | tf_op jit(solution)/shard_map/dot_general | solution.py:91
  334.2 0.0 reduce-scatter.2.cloned.1.call-update
  334.2 7.5 %multiply_convert_fusion = bf16[2,256,6144]{1,2,0:T(8,128)(2,1)} fusion(bf16[2,256,6144]{1,2,0:T(8,128)(2,1)} %all-gather.7.cloned.1.call-done, f32[2]{0:T(128)S(1)} %get-tuple-element.20), kind=kLoop, calls=%fused_computation | loop fusion | flops 9437184 | bytes 12582920 | tf_op jit(solution)/shard_map/convert_element_type | solution.py:86
  341.7 8.7 %copy.35 = bf16[2,256,6144]{2,1,0:T(8,128)(2,1)} copy(bf16[2,256,6144]{1,2,0:T(8,128)(2,1)} %multiply_convert_fusion) | data formatting | bytes 12582912 | tf_op jit(solution)/shard_map/convert_element_type | solution.py:86
  350.4 5.4 %convolution_convert_fusion = bf16[384,6144]{1,0:T(8,128)(2,1)S(1)} fusion(bf16[512,384]{1,0:T(8,128)(2,1)S(1)} %get-tuple-element.24, bf16[512,6144]{1,0:T(8,128)(2,1)} %bitcast.43), kind=kOutput, calls=%fused_computation.3 | convolution fusion | flops 2418278400 | bytes 11403264 | tf_op jit(solution)/shard_map/dot_general | solution.py:98
  355.8 2.6 copy.44
  358.4 4.9 %all-to-all-start.1 = ((bf16[4,384,1536]{2,1,0:T(8,128)(2,1)}), bf16[4,384,1536]{2,1,0:T(8,128)(2,1)}, u32[]{:S(2)}, u32[]{:S(2)}) async-start(bf16[4,384,1536]{2,1,0:T(8,128)(2,1)} %bitcast.44), calls=%async_computation.2 | async-start | bytes 9437184 | tf_op jit(solution)/shard_map/all_to_all | solution.py:36
  363.3 0.6 copy.38
  364.0 67.2 %all-to-all-done.1 = bf16[4,384,1536]{2,1,0:T(8,128)(2,1)} async-done(((bf16[4,384,1536]{2,1,0:T(8,128)(2,1)}), bf16[4,384,1536]{2,1,0:T(8,128)(2,1)}, u32[]{:S(2)}, u32[]{:S(2)}) %all-to-all-start.1) | async-done | bytes 4718624 | tf_op jit(solution)/shard_map/all_to_all | solution.py:36
  431.2 4.7 %convert_reduce_fusion = f32[384,1536]{1,0:T(8,128)} fusion(bf16[4,384,1536]{2,1,0:T(8,128)(2,1)} %all-to-all-done.1), kind=kLoop, calls=%fused_computation.2 | loop fusion | flops 4128768 | bytes 7077888 | tf_op jit(solution)/shard_map/reduce_sum | solution.py:37
  435.9 0.0 reduce-scatter.2.cloned.1.call-done
  435.9 2.7 copy.37
  (2 shorter events, 0.0 us)
Async XLA Ops:
  7.2 88.4 %all-gather.5.cloned.1.call-start = ((), (), s32[]{:S(2)}) async-start(), calls=%async_computation.3 | async-start | bytes 6389760 | tf_op jit(solution)/shard_map/all_gather | solution.py:52
  7.9 167.7 %all-gather.7.cloned.1.call-start = ((), (), s32[]{:S(2)}) async-start(), calls=%async_computation.4 | async-start | bytes 6389760 | tf_op jit(solution)/shard_map/all_gather | solution.py:59
  8.6 220.1 %all-gather.11.cloned.1.call-start = ((), (), s32[]{:S(2)}) async-start(), calls=%async_computation.6 | async-start | bytes 5898240 | tf_op jit(solution)/shard_map/all_gather | solution.py:56
  9.4 276.6 %all-gather.9.cloned.1.call-start = ((), (), s32[]{:S(2)}) async-start(), calls=%async_computation.5 | async-start | bytes 5898240 | tf_op jit(solution)/shard_map/all_gather | solution.py:63
  294.0 7.8 %slice-start = ((s8[6291456]{0:T(1024)(128)(4,1)}), s8[4194304]{0:T(1024)(128)(4,1)S(1)}, s32[]{:S(2)}) async-start(s8[6291456]{0:T(1024)(128)(4,1)} %bitcast.41), calls=%async_computation.8 | async-start | bytes 8388608
  294.4 7.4 %slice-start.1 = ((s8[6291456]{0:T(1024)(128)(4,1)}), s8[2097152]{0:T(1024)(128)(4,1)S(1)}, s32[]{:S(2)}) async-start(s8[6291456]{0:T(1024)(128)(4,1)} %bitcast.41), calls=%async_computation.9 | async-start | bytes 4194304
  301.8 23.7 %copy-start = (f32[2]{0:T(128)S(1)}, f32[2]{0:T(128)}, u32[]{:S(2)}) copy-start(f32[2]{0:T(128)} %param.9) | copy-start | bytes 28
  305.2 20.1 %all-to-all-start = ((f32[64,1,4]{2,1,0:T(1,128)}), f32[64,1,4]{2,1,0:T(1,128)S(1)}, u32[]{:S(2)}, u32[]{:S(2)}) async-start(f32[64,1,4]{2,1,0:T(1,128)} %broadcast_in_dim.4), calls=%async_computation | async-start | bytes 65536 | tf_op jit(solution)/shard_map/all_to_all | solution.py:12
  316.1 119.8 %reduce-scatter.2.cloned.1.call-start = ((), (), s32[]{:S(2)}) async-start(), calls=%async_computation.7 | async-start | bytes 5898240 | tf_op jit(solution)/shard_map/reduce_scatter | solution.py:90
  358.4 72.8 %all-to-all-start.1 = ((bf16[4,384,1536]{2,1,0:T(8,128)(2,1)}), bf16[4,384,1536]{2,1,0:T(8,128)(2,1)}, u32[]{:S(2)}, u32[]{:S(2)}) async-start(bf16[4,384,1536]{2,1,0:T(8,128)(2,1)} %bitcast.44), calls=%async_computation.2 | async-start | bytes 9437184 | tf_op jit(solution)/shard_map/all_to_all | solution.py:36
Sparse Core Ops, SparseCore 0:
  10.8 84.6 all-gather.4
  98.3 77.2 all-gather.6
  177.4 51.2 all-gather.10
  230.4 55.5 all-gather.8
  334.3 59.8 reduce-scatter.1
where the time goes:
time: 446 us; the launch traced here: 445 us
  waiting for transfers between devices  330 us (74%)
  matrix products  39.5 us (9%)
  local copies, waits for them, and re-layouts  32.9 us (7%)
  starting transfers between devices  16.1 us (4%)
  between operations  13.9 us (3%)
  other arithmetic  12.4 us (3%)
    all_gather x1, waiting for transfers between devices, on_device(): lax.all_gather(inputs, 'mp', axis=2, tiled=True).reshape(count_rows, -1)  85.6 us
    all_gather x1, waiting for transfers between devices, on_device(): lax.all_gather(cotangent, 'mp', axis=2, tiled=True).reshape(count_rows, -1)  71.4 us
    all_to_all x1, waiting for transfers between devices, sum_at_owner(): lax.all_to_all(pieces, axis, split_axis=0, concat_axis=0, tiled=True)  67.2 us
    all_gather x1, waiting for transfers between devices, on_device(): lax.all_gather(w_down, 'dp', axis=1, tiled=True)  50.3 us
    all_gather x1, waiting for transfers between devices, on_device(): lax.all_gather(w_up, 'dp', axis=0, tiled=True)  44.5 us
    all_to_all x1, starting transfers between devices, sent_to_all(): return lax.all_to_all(copies, axis, split_axis=0, concat_axis=0, tiled=True)  10.8 us
    dot_general x4, matrix products, gram_of(): jnp.einsum('btd,bsd->bts', cube, cube, preferred_element_type=jnp.float32)  10.8 us
  transfers between devices with their start and end apart: 7, of which 6 were waited for; matrix products, arithmetic and copies ran while one was open for 12% of the time, Pallas kernels for 0%

commit v1 on v0

--- a/solution.py
+++ b/solution.py
@@ -5,6 +5,11 @@
 
 inv_root_two = 0.7071067811865476
 inv_root_two_pi = 0.3989422804014327
+
+
+def gather_blocks(x, mesh_axis, dim):
+    shards = lax.all_gather(x, mesh_axis)
+    return jnp.concatenate(shards, axis=dim)
 
 
 def sent_to_all(shard, axis):
@@ -56,7 +61,7 @@
         columns, lax.all_gather(w_up, "dp", axis=0, tiled=True), preferred_element_type=jnp.float32
     )
     act = (pre * normal_cdf(pre)).astype(jnp.bfloat16)
-    dy_whole = lax.all_gather(cotangent, "mp", axis=2, tiled=True).reshape(count_rows, -1)
+    dy_whole = gather_blocks(cotangent, "mp", 2).reshape(count_rows, -1)
     columns = dy_whole
     dact = lax.dot_general(
         columns,

time: 446 us -> 446 us (level)
  other arithmetic: 12.4 us -> 4.91 us
  waiting for transfers between devices: 330 us -> 336 us
    all_gather x1, waiting for transfers between devices: 85.6 us -> 61.1 us  [on_device(): lax.all_gather(inputs, 'mp', axis=2, tiled=True).reshape(count_rows, -1)]
    all_to_all x1, waiting for transfers between devices: 67.2 us -> 83.3 us  [sum_at_owner(): lax.all_to_all(pieces, axis, split_axis=0, concat_axis=0, tiled=True)]
    reshape x0 -> x2, local copies, waits for them, and re-layouts: none -> 15.1 us  [gather_blocks(): return jnp.concatenate(shards, axis=dim)]
    all_gather x1, waiting for transfers between devices: 71.4 us -> 85.5 us  [gather_blocks(): shards = lax.all_gather(x, mesh_axis)]
    all_gather x1 -> x0, local copies, waits for them, and re-layouts: 8.68 us -> none  [on_device(): lax.all_gather(cotangent, 'mp', axis=2, tiled=True).reshape(count_rows, -1)]
    convert_element_type x1 -> x0, local copies, waits for them, and re-layouts: 8.68 us -> none  [on_device(): cot_clip = (factor[:, 1][:, None, None] * dy_whole.reshape(images, patche...]
    convert_element_type x1 -> x0, other arithmetic: 7.52 us -> none  [on_device(): cot_clip = (factor[:, 1][:, None, None] * dy_whole.reshape(images, patche...]
  transfers between devices with their start and end apart: 7 -> 7, of which waited for: 6 -> 6; matrix products, arithmetic and copies ran while one was open for 12% -> 11% of each run, Pallas kernels for 0% -> 0%
where the time goes in v1:
time: 446 us; the launch traced here: 445 us
  waiting for transfers between devices  336 us (75%)
  matrix products  39.9 us (9%)
  local copies, waits for them, and re-layouts  34.4 us (8%)
  starting transfers between devices  16 us (4%)
  between operations  13.9 us (3%)
  other arithmetic  4.91 us (1%)
    all_gather x1, waiting for transfers between devices, gather_blocks(): shards = lax.all_gather(x, mesh_axis)  85.5 us
    all_to_all x1, waiting for transfers between devices, sum_at_owner(): lax.all_to_all(pieces, axis, split_axis=0, concat_axis=0, tiled=True)  83.3 us
    all_gather x1, waiting for transfers between devices, on_device(): lax.all_gather(inputs, 'mp', axis=2, tiled=True).reshape(count_rows, -1)  61.1 us
    all_gather x1, waiting for transfers between devices, on_device(): lax.all_gather(w_down, 'dp', axis=1, tiled=True)  50.1 us
    all_gather x1, waiting for transfers between devices, on_device(): lax.all_gather(w_up, 'dp', axis=0, tiled=True)  44.5 us
    reshape x2, local copies, waits for them, and re-layouts, gather_blocks(): return jnp.concatenate(shards, axis=dim)  15.1 us
    all_to_all x1, starting transfers between devices, sent_to_all(): return lax.all_to_all(copies, axis, split_axis=0, concat_axis=0, tiled=True)  10.8 us
    dot_general x4, matrix products, gram_of(): jnp.einsum('btd,bsd->bts', cube, cube, preferred_element_type=jnp.float32)  10.7 us
  transfers between devices with their start and end apart: 7, of which 6 were waited for; matrix products, arithmetic and copies ran while one was open for 11% of the time, Pallas kernels for 0%

profile of v1, /device:TPU:1, one launch (start us, length us, event | category | flops | bytes accessed | tf_op | source)
XLA Modules:
  0.0 445.3 jit_solution(8081282076292831385)
XLA Ops:
  7.2 0.0 all-gather.12.cloned.1.call-start
  7.2 0.7 all-gather.12.cloned.1.call-update
  7.9 0.0 all-gather.6.cloned.1.call-start
  7.9 0.7 all-gather.6.cloned.1.call-update
  8.6 0.0 all-gather.10.cloned.1.call-start
  8.7 0.7 all-gather.10.cloned.1.call-update
  9.4 0.0 all-gather.8.cloned.1.call-start
  9.4 0.5 all-gather.8.cloned.1.call-update
  10.0 85.5 %all-gather.12.cloned.1.call-done = bf16[128,256,96]{1,2,0:T(8,128)(2,1)} async-done(((bf16[2,256,96]{1,2,0:T(8,128)(2,1)}), bf16[128,256,96]{1,2,0:T(8,128)(2,1)}) %all-gather.12.cloned.1.call-update) | async-done | bytes 6291472 | tf_op jit(solution)/shard_map/all_gather | solution.py:11
  95.4 0.0 copy-start
  95.5 12.1 %copy.45 = bf16[2,256,64,96]{1,0,3,2:T(2,128)(2,1)S(1)} copy(bf16[2,256,64,96]{1,3,0,2:T(8,128)(2,1)} %bitcast.53) | data formatting | bytes 12582912 | tf_op jit(solution)/shard_map/reshape | solution.py:12
  107.5 0.0 copy-done
  107.6 3.0 copy.47
  110.6 3.8 copy.61
  114.4 61.1 %all-gather.6.cloned.1.call-done = bf16[2,256,6144]{1,2,0:T(8,128)(2,1)} async-done(((bf16[2,256,96]{1,2,0:T(8,128)(2,1)}), bf16[2,256,6144]{1,2,0:T(8,128)(2,1)}) %all-gather.6.cloned.1.call-update) | async-done | bytes 6291472 | tf_op jit(solution)/shard_map/all_gather | solution.py:57
  175.5 8.6 %copy.46 = bf16[2,256,6144]{2,1,0:T(8,128)(2,1)} copy(bf16[2,256,6144]{1,2,0:T(8,128)(2,1)} %all-gather.6.cloned.1.call-done) | data formatting | bytes 12582912 | tf_op jit(solution)/shard_map/all_gather | solution.py:57
  184.1 44.5 %all-gather.10.cloned.1.call-done = bf16[6144,384]{1,0:T(8,128)(2,1)} async-done(((bf16[1536,384]{1,0:T(8,128)(2,1)}), bf16[6144,384]{1,0:T(8,128)(2,1)}) %all-gather.10.cloned.1.call-update) | async-done | bytes 4718608 | tf_op jit(solution)/shard_map/all_gather | solution.py:61
  228.6 7.1 %multiply_convert_fusion.3 = (bf16[512,384]{1,0:T(8,128)(2,1)S(1)}, f32[512,384]{1,0:T(8,128)S(1)}) fusion(bf16[512,6144]{1,0:T(8,128)(2,1)} %bitcast.59, bf16[6144,384]{1,0:T(8,128)(2,1)} %all-gather.10.cloned.1.call-done), kind=kOutput, calls=%fused_computation.19 | convolution fusion | flops 2416902144 | bytes 12189696 | tf_op jit(solution)/shard_map/dot_general | solution.py:60
  235.8 50.1 %all-gather.8.cloned.1.call-done = bf16[384,6144]{1,0:T(8,128)(2,1)} async-done(((bf16[384,1536]{1,0:T(8,128)(2,1)}), bf16[384,6144]{1,0:T(8,128)(2,1)}) %all-gather.8.cloned.1.call-update) | async-done | bytes 4718608 | tf_op jit(solution)/shard_map/all_gather | solution.py:68
  285.9 7.7 %fusion.2 = bf16[512,384]{1,0:T(8,128)(2,1)S(1)} fusion(bf16[512,6144]{0,1:T(8,128)(2,1)} %bitcast.57, bf16[384,6144]{1,0:T(8,128)(2,1)} %all-gather.8.cloned.1.call-done, f32[512,384]{1,0:T(8,128)S(1)} %get-tuple-element.28), kind=kOutput, calls=%fused_computation.8 | convolution fusion | flops 2417885184 | bytes 12189696 | tf_op jit(solution)/shard_map/dot_general | solution.py:66
  293.6 0.3 fusion.10
  293.9 0.0 slice-start
  293.9 0.3 fusion.11
  294.3 0.0 slice-start.1
  294.3 7.4 %fusion.4 = f32[2]{0:T(128)S(1)} fusion(f32[2,256,256]{2,1,0:T(8,128)S(1)} %fusion.11, bf16[2,256,6144]{1,2,0:T(8,128)(2,1)} %bitcast.52), kind=kOutput, calls=%fused_computation.13 | convolution fusion | flops 1610874880 | bytes 6815752 | tf_op jit(solution)/shard_map/btd,bsd->bts/dot_general | solution.py:51
  301.7 0.0 slice-done
  301.7 0.0 slice-done.1
  301.7 0.0 copy-start.1
  301.7 2.7 fusion.3
  304.4 0.1 pad_maximum_fusion.1
  304.5 0.6 broadcast_in_dim.4
  305.1 10.8 %all-to-all-start = ((f32[64,1,4]{2,1,0:T(1,128)}), f32[64,1,4]{2,1,0:T(1,128)S(1)}, u32[]{:S(2)}, u32[]{:S(2)}) async-start(f32[64,1,4]{2,1,0:T(1,128)} %broadcast_in_dim.4), calls=%async_computation | async-start | bytes 65536 | tf_op jit(solution)/shard_map/all_to_all | solution.py:17
  316.0 0.0 reduce-scatter.2.cloned.1.call-start
  316.0 0.2 copy.51
  316.2 9.0 %all-to-all-done = f32[64,1,4]{2,1,0:T(1,128)S(1)} async-done(((f32[64,1,4]{2,1,0:T(1,128)}), f32[64,1,4]{2,1,0:T(1,128)S(1)}, u32[]{:S(2)}, u32[]{:S(2)}) %all-to-all-start) | async-done | bytes 1056 | tf_op jit(solution)/shard_map/all_to_all | solution.py:17
  325.2 0.1 reduce_sum.38
  325.3 0.1 sqrt_bitcast_fusion.1
  325.4 0.0 copy-done.1
  325.4 0.1 pad_maximum_fusion
  325.4 8.8 %fusion = bf16[6144,384]{0,1:T(8,128)(2,1)} fusion(bf16[2,256,6144]{1,2,0:T(8,128)(2,1)} %all-gather.6.cloned.1.call-done, bf16[2,256,384]{1,2,0:T(8,128)(2,1)S(1)} %copy.51, f32[2]{0:T(128)S(1)} %get-tuple-element.24), kind=kOutput, calls=%fused_computation.4 | convolution fusion | flops 2418868224 | bytes 11403272 | tf_op jit(solution)/shard_map/dot_general | solution.py:96
  334.3 0.0 reduce-scatter.2.cloned.1.call-update
  334.3 0.1 broadcast_bitcast_fusion
  334.4 5.5 %convolution_convert_fusion = bf16[384,6144]{1,0:T(8,128)(2,1)S(1)} fusion(bf16[512,384]{1,0:T(8,128)(2,1)S(1)} %get-tuple-element.27, bf16[512,6144]{0,1:T(8,128)(2,1)} %bitcast.58, f32[512]{0:T(512)S(1)} %bitcast.64), kind=kOutput, calls=%fused_computation.3 | convolution fusion | flops 2427715584 | bytes 11405312 | tf_op jit(solution)/shard_map/dot_general | solution.py:103
  339.8 2.5 copy.64
  342.4 5.0 %all-to-all-start.1 = ((bf16[4,384,1536]{2,1,0:T(8,128)(2,1)}), bf16[4,384,1536]{2,1,0:T(8,128)(2,1)}, u32[]{:S(2)}, u32[]{:S(2)}) async-start(bf16[4,384,1536]{2,1,0:T(8,128)(2,1)} %bitcast.56), calls=%async_computation.2 | async-start | bytes 9437184 | tf_op jit(solution)/shard_map/all_to_all | solution.py:41
  347.4 0.6 copy.54
  348.0 83.3 %all-to-all-done.1 = bf16[4,384,1536]{2,1,0:T(8,128)(2,1)} async-done(((bf16[4,384,1536]{2,1,0:T(8,128)(2,1)}), bf16[4,384,1536]{2,1,0:T(8,128)(2,1)}, u32[]{:S(2)}, u32[]{:S(2)}) %all-to-all-start.1) | async-done | bytes 4718624 | tf_op jit(solution)/shard_map/all_to_all | solution.py:41
  431.3 4.7 %convert_reduce_fusion = f32[384,1536]{1,0:T(8,128)} fusion(bf16[4,384,1536]{2,1,0:T(8,128)(2,1)} %all-to-all-done.1), kind=kLoop, calls=%fused_computation.2 | loop fusion | flops 4128768 | bytes 7077888 | tf_op jit(solution)/shard_map/reduce_sum | solution.py:42
  436.0 0.0 reduce-scatter.2.cloned.1.call-done
  436.0 2.7 copy.53
  (3 shorter events, 0.0 us)
Async XLA Ops:
  7.2 88.3 %all-gather.12.cloned.1.call-start = ((), (), s32[]{:S(2)}) async-start(), calls=%async_computation.7 | async-start | bytes 6389760 | tf_op jit(solution)/shard_map/all_gather | solution.py:11
  7.9 167.6 %all-gather.6.cloned.1.call-start = ((), (), s32[]{:S(2)}) async-start(), calls=%async_computation.3 | async-start | bytes 6389760 | tf_op jit(solution)/shard_map/all_gather | solution.py:57
  8.6 220.0 %all-gather.10.cloned.1.call-start = ((), (), s32[]{:S(2)}) async-start(), calls=%async_computation.5 | async-start | bytes 5898240 | tf_op jit(solution)/shard_map/all_gather | solution.py:61
  9.4 276.5 %all-gather.8.cloned.1.call-start = ((), (), s32[]{:S(2)}) async-start(), calls=%async_computation.4 | async-start | bytes 5898240 | tf_op jit(solution)/shard_map/all_gather | solution.py:68
  95.4 12.1 %copy-start = (bf16[128,256,96]{1,2,0:T(8,128)(2,1)S(1)}, bf16[128,256,96]{1,2,0:T(8,128)(2,1)}, u32[]{:S(2)}) copy-start(bf16[128,256,96]{1,2,0:T(8,128)(2,1)} %all-gather.12.cloned.1.call-done) | copy-start | bytes 18874372
  293.9 7.8 %slice-start = ((s8[6291456]{0:T(1024)(128)(4,1)}), s8[4194304]{0:T(1024)(128)(4,1)S(1)}, s32[]{:S(2)}) async-start(s8[6291456]{0:T(1024)(128)(4,1)} %bitcast.50), calls=%async_computation.8 | async-start | bytes 8388608
  294.3 7.4 %slice-start.1 = ((s8[6291456]{0:T(1024)(128)(4,1)}), s8[2097152]{0:T(1024)(128)(4,1)S(1)}, s32[]{:S(2)}) async-start(s8[6291456]{0:T(1024)(128)(4,1)} %bitcast.50), calls=%async_computation.9 | async-start | bytes 4194304
  301.7 23.7 %copy-start.1 = (f32[2]{0:T(128)S(1)}, f32[2]{0:T(128)}, u32[]{:S(2)}) copy-start(f32[2]{0:T(128)} %param.9) | copy-start | bytes 28
  305.1 20.1 %all-to-all-start = ((f32[64,1,4]{2,1,0:T(1,128)}), f32[64,1,4]{2,1,0:T(1,128)S(1)}, u32[]{:S(2)}, u32[]{:S(2)}) async-start(f32[64,1,4]{2,1,0:T(1,128)} %broadcast_in_dim.4), calls=%async_computation | async-start | bytes 65536 | tf_op jit(solution)/shard_map/all_to_all | solution.py:17
  316.0 120.1 %reduce-scatter.2.cloned.1.call-start = ((), (), s32[]{:S(2)}) async-start(), calls=%async_computation.6 | async-start | bytes 5898240 | tf_op jit(solution)/shard_map/reduce_scatter | solution.py:95
  342.4 88.9 %all-to-all-start.1 = ((bf16[4,384,1536]{2,1,0:T(8,128)(2,1)}), bf16[4,384,1536]{2,1,0:T(8,128)(2,1)}, u32[]{:S(2)}, u32[]{:S(2)}) async-start(bf16[4,384,1536]{2,1,0:T(8,128)(2,1)} %bitcast.56), calls=%async_computation.2 | async-start | bytes 9437184 | tf_op jit(solution)/shard_map/all_to_all | solution.py:41
Sparse Core Ops, SparseCore 0:
  10.7 84.6 all-gather.11
  98.3 77.1 all-gather.5
  177.3 51.2 all-gather.9
  230.3 55.5 all-gather.7
  334.4 75.6 reduce-scatter.1
